TPU v7x, 32 devices: a whole 2x2x4 slice. The times are simulated.
32 devices in a mesh: point: 8 (over y, x, core), batch: 4 (over z).
Axes of the slice: x: 2, y: 2, z: 4, core: 2. Of those that a mesh axis runs over, the one named last changes fastest.
Arguments:
- activations: bfloat16 [128, 14, 14, 1024], P('batch'), may hold values from -8 to 8
- labels: int32 [128], P('batch'), may hold values from 0 to 999
- t_values: float32 [64], replicated, may hold values from 0 to 1
- point_index: int32 [8], replicated, may hold values from 0 to 63
- w_reduce: bfloat16 [3, 1024, 256], P(None, 'point'), may hold values from -1 to 1
- w_spatial: bfloat16 [3, 2304, 256], P(None, 'point'), may hold values from -0.125 to 0.125
- w_expand: bfloat16 [3, 256, 1024], P(None, 'point'), may hold values from -0.375 to 0.375
- w_classes: bfloat16 [3, 1000, 1024], P(None, None, 'point'), may hold values from -0.1875 to 0.1875
- norm_gain: float32 [3, 1536], replicated, may hold values from 0.5 to 1.5
- norm_bias: float32 [3, 1536], replicated, may hold values from -3 to 3
- class_bias: float32 [3, 1000], replicated, may hold values from -3 to 3
Outputs:
- mean_reduce: float32 [8, 256], P('point')
- var_reduce: float32 [8, 256], P('point')
- mean_spatial: float32 [8, 256], P('point')
- var_spatial: float32 [8, 256], P('point')
- mean_expand: float32 [8, 1024], P('point')
- var_expand: float32 [8, 1024], P('point')
- margin: float32 [8], replicated
All inputs are finite; a program needn't handle non-finite values.
Results may differ from a plain program's by a relative error of at most 0.003.
Values may be sent and summed in bfloat16 or wider, within the bound.
A program may use at most 128 MiB of HBM per device.

v0:
```python
import jax
import jax.numpy as jnp
from jax import lax
from jax.sharding import PartitionSpec as P

EPSILON = 1e-05


def curve_coefficients(t_values, point_index):
    table_size = t_values.shape[0]
    matches = point_index[:, None] == jnp.arange(table_size, dtype=jnp.int32)[None, :]
    picked = jnp.sum(jnp.where(matches, t_values[None, :], 0.0), axis=1)
    doubled = 2.0 * picked
    return jnp.stack(
        [
            jnp.maximum(1.0 - doubled, 0.0),
            1.0 - jnp.abs(1.0 - doubled),
            jnp.maximum(doubled - 1.0, 0.0),
        ],
        axis=1,
    )


def blend_all(coefficients, endpoints):
    target_shape = (coefficients.shape[0],) + (1,) * (endpoints.ndim - 1)
    start_part = coefficients[:, 0].reshape(target_shape) * endpoints[0].astype(jnp.float32)[None]
    bend_part = coefficients[:, 1].reshape(target_shape) * endpoints[1].astype(jnp.float32)[None]
    final_part = coefficients[:, 2].reshape(target_shape) * endpoints[2].astype(jnp.float32)[None]
    return start_part + bend_part + final_part


def point_weight(endpoints, own_row, by_columns):
    if by_columns:
        gathered = lax.all_gather(endpoints, "point", axis=2, tiled=True)
    else:
        gathered = lax.all_gather(endpoints, "point", axis=1, tiled=True)
    return blend_all(own_row, gathered)[0].astype(jnp.bfloat16)


def map_product(maps, kernel):
    return lax.dot_general(
        maps, kernel, (((3,), (0,)), ((), ())), preferred_element_type=jnp.float32
    )


def batch_norm(pre_norm, gain_part, bias_part, row_count):
    channel_total, channel_squares = lax.psum(
        (jnp.sum(pre_norm, axis=(0, 1, 2)), jnp.sum(pre_norm * pre_norm, axis=(0, 1, 2))), "batch"
    )
    channel_mean = channel_total / row_count
    channel_var = channel_squares / row_count - channel_mean * channel_mean
    scaled = (pre_norm - channel_mean) * lax.rsqrt(channel_var + EPSILON) * gain_part + bias_part
    return (channel_mean, channel_var, scaled)


def spatial_conv(source, kernel):
    side_len = source.shape[1]
    middle = source.shape[3]
    padded = jnp.pad(source, ((0, 0), (1, 1), (1, 1), (0, 0)))
    widened = jnp.concatenate(
        [
            padded[:, :, 0:side_len, :],
            padded[:, :, 1 : side_len + 1, :],
            padded[:, :, 2 : side_len + 2, :],
        ],
        axis=3,
    )
    summed = map_product(widened[:, 0:side_len], kernel[0 : 3 * middle])
    summed = summed + map_product(widened[:, 1 : side_len + 1], kernel[3 * middle : 6 * middle])
    summed = summed + map_product(widened[:, 2 : side_len + 2], kernel[6 * middle : 9 * middle])
    return summed


def shards(
    activations,
    labels,
    t_values,
    point_index,
    w_reduce,
    w_spatial,
    w_expand,
    w_classes,
    norm_gain,
    norm_bias,
    class_bias,
):
    coefficients = curve_coefficients(t_values, point_index)
    own_row = lax.dynamic_slice_in_dim(coefficients, lax.axis_index("point"), 1, 0)
    reduce_w = point_weight(w_reduce, own_row, False)
    spatial_w = point_weight(w_spatial, own_row, False)
    expand_w = point_weight(w_expand, own_row, False)
    class_w = point_weight(w_classes, own_row, True)
    gain_now = blend_all(own_row, norm_gain)[0]
    bias_now = blend_all(own_row, norm_bias)[0]
    shift_now = blend_all(own_row, class_bias)[0]
    images, side_len, _, channels = activations.shape
    middle = w_reduce.shape[2]
    row_count = float(images * side_len * side_len * lax.axis_size("batch"))
    reduced = map_product(activations, reduce_w)
    mean_one, var_one, normed_one = batch_norm(
        reduced, gain_now[:middle], bias_now[:middle], row_count
    )
    first = jax.nn.relu(normed_one).astype(jnp.bfloat16)
    spatial = spatial_conv(first, spatial_w)
    mean_two, var_two, normed_two = batch_norm(
        spatial, gain_now[middle : 2 * middle], bias_now[middle : 2 * middle], row_count
    )
    second = jax.nn.relu(normed_two).astype(jnp.bfloat16)
    expanded = map_product(second, expand_w)
    mean_three, var_three, normed_three = batch_norm(
        expanded, gain_now[2 * middle :], bias_now[2 * middle :], row_count
    )
    block_out = jax.nn.relu(normed_three + activations.astype(jnp.float32))
    pooled = jnp.mean(block_out, axis=(1, 2)).astype(jnp.bfloat16)
    logits = (
        lax.dot_general(
            pooled, class_w, (((1,), (1,)), ((), ())), preferred_element_type=jnp.float32
        )
        + shift_now
    )
    classes = logits.shape[1]
    onehot = labels[:, None] == jnp.arange(classes, dtype=jnp.int32)[None, :]
    correct = jnp.sum(jnp.where(onehot, logits, 0.0), axis=1)
    rivals = jnp.max(jnp.where(onehot, -1e30, logits), axis=1)
    partial_value = jnp.sum(correct - rivals) / (images * lax.axis_size("batch"))
    point_count = point_index.shape[0]
    placed = jnp.where(
        jnp.arange(point_count, dtype=jnp.int32) == lax.axis_index("point"), partial_value, 0.0
    )
    margin_all = lax.psum(placed, ("point", "batch"))
    return (
        mean_one[None],
        var_one[None],
        mean_two[None],
        var_two[None],
        mean_three[None],
        var_three[None],
        margin_all,
    )


def solution(mesh):
    placed = (
        P("batch", None, None, None),
        P("batch"),
        P(),
        P(),
        P(None, "point", None),
        P(None, "point", None),
        P(None, "point", None),
        P(None, None, "point"),
        P(),
        P(),
        P(),
    )
    return jax.shard_map(
        shards,
        mesh=mesh,
        in_specs=placed,
        out_specs=(
            P("point", None),
            P("point", None),
            P("point", None),
            P("point", None),
            P("point", None),
            P("point", None),
            P(),
        ),
        check_vma=False,
    )
```

profile of v0, /device:TPU:0, one launch (start us, length us, event | category | flops | bytes accessed | tf_op | source)
XLA Modules:
  0.0 208.5 jit_solution(10090536275269189656)
XLA Ops:
  7.2 0.7 all-gather.5.cloned.1.call-update
  7.9 0.7 all-gather.7.cloned.1.call-update
  8.7 0.7 all-gather.9.cloned.1.call-update
  10.0 0.9 select_reduce_fusion.2
  11.5 2.8 %multiply_add_fusion = (f32[1,1536]{1,0:T(1,128)S(1)}, f32[1,1536]{1,0:T(1,128)S(1)}) fusion(f32[3,1536]{1,0:T(4,128)} %param.20, f32[]{:T(128)} %bitcast.5, f32[]{:T(128)} %bitcast.4, f32[]{:T(128)} %bitcast.3, f32[3,1536]{1,0:T(4,128)} %param.19), kind=kLoop, calls=%fused_computation.50 | loop fusion | flops 15360 | bytes 49164 | tf_op jit(solution)/shard_map/add | solution.py:29
  14.3 2.7 %multiply_add_fusion.2 = f32[1,1000]{1,0:T(1,128)S(1)} fusion(f32[3,1000]{1,0:T(4,128)} %param.21, f32[]{:T(128)} %bitcast.5, f32[]{:T(128)} %bitcast.4, f32[]{:T(128)} %bitcast.3), kind=kLoop, calls=%fused_computation.52 | loop fusion | flops 5000 | bytes 16012 | tf_op jit(solution)/shard_map/add | solution.py:29
  17.0 21.2 %all-gather.5.cloned.1.call-done = bf16[3,1024,256]{2,1,0:T(8,128)(2,1)} async-done(((bf16[3,128,256]{2,1,0:T(8,128)(2,1)}), bf16[3,1024,256]{2,1,0:T(8,128)(2,1)}) %all-gather.5.cloned.1.call-update) | async-done | bytes 1572880 | tf_op jit(solution)/shard_map/all_gather | solution.py:36
  38.2 13.3 %multiply_reduce_fusion.2 = (f32[256]{0:T(256)S(1)}, f32[256]{0:T(256)S(1)}, f32[256,32,14,14]{0,1,3,2:T(8,128)}) fusion(bf16[32,14,14,1024]{3,0,2,1:T(8,128)(2,1)} %param.11, bf16[3,1024,256]{2,1,0:T(8,128)(2,1)} %all-gather.5.cloned.1.call-done, f32[]{:T(128)} %bitcast.5, f32[]{:T(128)} %bitcast.4, f32[]{:T(128)} %bitcast.3), kind=kOutput, calls=%fused_computation.7 | convolution fusion | flops 3295510016 | bytes 20842508 | tf_op jit(solution)/shard_map/dot_general | solution.py:41
  51.5 11.7 %all-reduce.3 = (f32[256]{0:T(256)S(1)}, f32[256]{0:T(256)S(1)}) all-reduce(f32[256]{0:T(256)S(1)} %get-tuple-element.12, f32[256]{0:T(256)S(1)} %get-tuple-element.11), channel_id=1, replica_groups=mesh['point'=8,'batch'=4] {'batch'}, use_global_device_ids=true, to_apply=%region_2.3 | all-reduce | flops 512 | bytes 4096 | tf_op jit(solution)/shard_map/psum | solution.py:47
  63.8 4.1 %fusion.1 = bf16[32,14,14,256]{3,0,2,1:T(8,128)(2,1)S(1)} fusion(f32[256,32,14,14]{0,1,3,2:T(8,128)} %get-tuple-element.43, f32[256]{0:T(256)S(1)} %bitcast.77, f32[256]{0:T(256)S(1)} %bitcast.78, f32[256]{0:T(256)S(1)} %get-tuple-element.25, f32[256]{0:T(256)S(1)} %get-tuple-element.39), kind=kLoop, calls=%fused_computation.13 | loop fusion | flops 9633792 | bytes 9637888 | tf_op jit(solution)/shard_map/convert_element_type | solution.py:103
  67.9 4.9 %pad_slice_fusion.2 = (bf16[32,16,14,256]{3,0,2,1:T(8,128)(2,1)}, bf16[32,16,14,256]{3,0,2,1:T(8,128)(2,1)}, bf16[32,16,14,256]{3,0,2,1:T(8,128)(2,1)}) fusion(bf16[32,14,14,256]{3,0,2,1:T(8,128)(2,1)S(1)} %fusion.1), kind=kLoop, calls=%fused_computation.10 | loop fusion | bytes 14221312 | tf_op jit(solution)/shard_map/slice | solution.py:62
  72.8 1.2 all-gather.7.cloned.1.call-done
  74.0 4.5 %add_convert_fusion.1 = bf16[1,2304,256]{2,1,0:T(8,128)(2,1)S(1)} fusion(bf16[3,2304,256]{2,1,0:T(8,128)(2,1)} %all-gather.7.cloned.1.call-done, f32[]{:T(128)} %bitcast.5, f32[]{:T(128)} %bitcast.4, f32[]{:T(128)} %bitcast.3), kind=kLoop, calls=%fused_computation.19 | loop fusion | flops 5308416 | bytes 4718604 | tf_op jit(solution)/shard_map/convert_element_type | solution.py:37
  78.5 7.3 %fusion.31 = f32[32,14,14,256]{3,0,2,1:T(8,128)} fusion(bf16[1,2304,256]{2,1,0:T(8,128)(2,1)S(1)} %add_convert_fusion.1, bf16[32,16,14,256]{3,0,2,1:T(8,128)(2,1)} %get-tuple-element.29, bf16[32,16,14,256]{3,0,2,1:T(8,128)(2,1)} %get-tuple-element.28, bf16[32,16,14,256]{3,0,2,1:T(8,128)(2,1)} %get-tuple-element.27), kind=kOutput, calls=%fused_computation.44 | convolution fusion | flops 2499280896 | bytes 17825792 | tf_op jit(solution)/shard_map/dot_general | solution.py:41
  85.8 1.2 copy-done.1
  87.0 1.0 copy-done.2
  88.0 5.4 %fusion.30 = f32[32,14,14,256]{3,0,2,1:T(8,128)} fusion(bf16[1,2304,256]{2,1,0:T(8,128)(2,1)S(1)} %add_convert_fusion.1, bf16[32,16,14,256]{3,0,2,1:T(8,128)(2,1)S(1)} %copy-done.2, bf16[32,16,14,256]{3,0,2,1:T(8,128)(2,1)S(1)} %copy-done.1, bf16[32,16,14,256]{3,0,2,1:T(8,128)(2,1)S(1)} %copy-done), kind=kOutput, calls=%fused_computation.42 | convolution fusion | flops 2499280896 | bytes 17825792 | tf_op jit(solution)/shard_map/dot_general | solution.py:41
  93.4 9.0 %multiply_reduce_fusion.1 = (f32[256]{0:T(256)S(1)}, f32[256]{0:T(256)S(1)}, f32[32,14,14,256]{3,0,2,1:T(8,128)}) fusion(bf16[1,2304,256]{2,1,0:T(8,128)(2,1)S(1)} %add_convert_fusion.1, bf16[32,16,14,256]{3,0,2,1:T(8,128)(2,1)S(1)} %copy-done.2, bf16[32,16,14,256]{3,0,2,1:T(8,128)(2,1)S(1)} %copy-done.1, bf16[32,16,14,256]{3,0,2,1:T(8,128)(2,1)S(1)} %copy-done, ...), kind=kOutput, calls=%fused_computation.5 | convolution fusion | flops 2507308544 | bytes 30672896 | tf_op jit(solution)/shard_map/dot_general | solution.py:41
  102.4 11.9 %all-reduce.2 = (f32[256]{0:T(256)S(1)}, f32[256]{0:T(256)S(1)}) all-reduce(f32[256]{0:T(256)S(1)} %get-tuple-element.10, f32[256]{0:T(256)S(1)} %get-tuple-element.9), channel_id=1, replica_groups=mesh['point'=8,'batch'=4] {'batch'}, use_global_device_ids=true, to_apply=%region_6.7 | all-reduce | flops 512 | bytes 4096 | tf_op jit(solution)/shard_map/psum | solution.py:47
  114.9 16.0 %multiply_reduce_fusion = (f32[1024]{0:T(1024)S(1)}, f32[1024]{0:T(1024)S(1)}, f32[32,14,14,1024]{3,0,2,1:T(8,128)}) fusion(bf16[3,256,1024]{2,1,0:T(8,128)(2,1)} %all-gather.9.cloned.1.call-done, f32[]{:T(128)} %bitcast.5, f32[]{:T(128)} %bitcast.4, f32[]{:T(128)} %bitcast.3, f32[32,14,14,256]{3,0,2,1:T(8,128)} %get-tuple-element.44, f32[256]{0:T(256)S(1)} %bitcast.84, ...), kind=kOutput, calls=%fused_computation.1 | convolution fusion | flops 3319592960 | bytes 33697804 | tf_op jit(solution)/shard_map/dot_general | solution.py:41
  130.9 8.5 %all-reduce.1 = (f32[1024]{0:T(1024)S(1)}, f32[1024]{0:T(1024)S(1)}) all-reduce(f32[1024]{0:T(1024)S(1)} %get-tuple-element.8, f32[1024]{0:T(1024)S(1)} %get-tuple-element.7), channel_id=1, replica_groups=mesh['point'=8,'batch'=4] {'batch'}, use_global_device_ids=true, to_apply=%region_10.11 | all-reduce | flops 2048 | bytes 16384 | tf_op jit(solution)/shard_map/psum | solution.py:47
  140.1 14.9 %maximum_reduce_fusion = f32[32,1024]{1,0:T(8,128)S(1)} fusion(bf16[32,14,14,1024]{3,0,2,1:T(8,128)(2,1)} %param.11, f32[32,14,14,1024]{3,0,2,1:T(8,128)} %get-tuple-element.45, f32[1024]{0:T(1024)S(1)} %bitcast.74, f32[1024]{0:T(1024)S(1)} %bitcast.75, f32[1024]{0:T(1024)S(1)} %get-tuple-element.21, f32[1024]{0:T(1024)S(1)} %get-tuple-element.34), kind=kLoop, calls=%fused_computation | loop fusion | flops 51347456 | bytes 38682624 | tf_op jit(solution)/shard_map/reduce_sum | solution.py:114
  155.0 6.1 %select_reduce_fusion = (f32[32]{0:T(128)S(1)}, f32[32]{0:T(128)S(1)}) fusion(s32[32]{0:T(128)S(1)} %copy-done.6, f32[1000]{0:T(1024)S(1)} %bitcast.80, bf16[3,1000,1024]{2,1,0:T(8,128)(2,1)} %all-gather.11.cloned.1.call-done, f32[]{:T(128)} %bitcast.5, f32[]{:T(128)} %bitcast.4, f32[]{:T(128)} %bitcast.3, f32[32,1024]{1,0:T(8,128)S(1)} %maximum_reduce_fusion), kind=kOutput, calls=%fused_computation.45 | convolution fusion | flops 75009472 | bytes 6279468 | tf_op jit(solution)/shard_map/dot_general | solution.py:116
  162.4 39.6 %psum.55 = f32[8]{0:T(128)} all-reduce(f32[8]{0:T(128)S(1)} %compare_select_fusion), channel_id=1, replica_groups=mesh['point'=8,'batch'=4] {'point','batch'}, use_global_device_ids=true, to_apply=%region_17.18 | all-reduce | flops 8 | bytes 64 | tf_op jit(solution)/shard_map/psum | solution.py:130
  (32 shorter events, 3.7 us)
Async XLA Ops:
  7.2 31.0 %all-gather.5.cloned.1.call-start = ((), (), s32[]{:S(2)}) async-start(), calls=%async_computation | async-start | bytes 1769472 | tf_op jit(solution)/shard_map/all_gather | solution.py:36
  7.9 66.1 %all-gather.7.cloned.1.call-start = ((), (), s32[]{:S(2)}) async-start(), calls=%async_computation.1 | async-start | bytes 3981312 | tf_op jit(solution)/shard_map/all_gather | solution.py:36
  8.7 106.3 %all-gather.9.cloned.1.call-start = ((), (), s32[]{:S(2)}) async-start(), calls=%async_computation.2 | async-start | bytes 1769472 | tf_op jit(solution)/shard_map/all_gather | solution.py:36
  9.4 145.6 %all-gather.11.cloned.1.call-start = ((), (), s32[]{:S(2)}) async-start(), calls=%async_computation.3 | async-start | bytes 6912000 | tf_op jit(solution)/shard_map/all_gather | solution.py:34
  63.8 9.0 %copy-start.4 = (f32[256]{0:T(256)}, f32[256]{0:T(256)S(1)}, u32[]{:S(2)}) copy-start(f32[256]{0:T(256)S(1)} %get-tuple-element.39) | copy-start | bytes 3076
  78.5 7.3 %copy-start = (bf16[32,16,14,256]{3,0,2,1:T(8,128)(2,1)S(1)}, bf16[32,16,14,256]{3,0,2,1:T(8,128)(2,1)}, u32[]{:S(2)}) copy-start(bf16[32,16,14,256]{3,0,2,1:T(8,128)(2,1)} %get-tuple-element.27) | copy-start | bytes 11010052
  78.5 8.5 %copy-start.1 = (bf16[32,16,14,256]{3,0,2,1:T(8,128)(2,1)S(1)}, bf16[32,16,14,256]{3,0,2,1:T(8,128)(2,1)}, u32[]{:S(2)}) copy-start(bf16[32,16,14,256]{3,0,2,1:T(8,128)(2,1)} %get-tuple-element.28) | copy-start | bytes 11010052
  78.5 9.5 %copy-start.2 = (bf16[32,16,14,256]{3,0,2,1:T(8,128)(2,1)S(1)}, bf16[32,16,14,256]{3,0,2,1:T(8,128)(2,1)}, u32[]{:S(2)}) copy-start(bf16[32,16,14,256]{3,0,2,1:T(8,128)(2,1)} %get-tuple-element.29) | copy-start | bytes 11010052
  114.9 16.0 %copy-start.5 = (f32[256]{0:T(256)}, f32[256]{0:T(256)S(1)}, u32[]{:S(2)}) copy-start(f32[256]{0:T(256)S(1)} %get-tuple-element.38) | copy-start | bytes 3076
  140.1 14.9 %copy-start.3 = (f32[1024]{0:T(1024)}, f32[1024]{0:T(1024)S(1)}, u32[]{:S(2)}) copy-start(f32[1024]{0:T(1024)S(1)} %get-tuple-element.34) | copy-start | bytes 12292
  140.1 14.9 %copy-start.6 = (s32[32]{0:T(128)S(1)}, s32[32]{0:T(128)}, u32[]{:S(2)}) copy-start(s32[32]{0:T(128)} %param.12) | copy-start | bytes 388
Sparse Core Ops, SparseCore 0:
  9.9 28.2 all-gather.4
  40.1 33.8 all-gather.6
  75.9 25.5 all-gather.8
  103.2 45.9 all-gather.10
where the time goes:
time: 209 us; the launch traced here: 208 us
  blocking collectives  71.7 us (34%)
  matrix products  57.1 us (27%)
  other arithmetic  32.2 us (15%)
  waiting for transfers between devices  24.9 us (12%)
  between operations  14.6 us (7%)
  local copies, waits for them, and re-layouts  7.82 us (4%)
    dot_general x5, matrix products, map_product(): lax.dot_general(maps, kernel, (((3,), (0,)), ((), ())), preferred_element...  51 us
    psum x1, blocking collectives, shards(): margin_all = lax.psum(placed, ('point', 'batch'))  39.6 us
    psum x3, blocking collectives, batch_norm(): lax.psum((jnp.sum(pre_norm, axis=(0, 1, 2)), jnp.sum(pre_norm * pre_norm,...  32.1 us
    all_gather x3, waiting for transfers between devices, point_weight(): gathered = lax.all_gather(endpoints, 'point', axis=1, tiled=True)  22.3 us
    reduce_sum x1, other arithmetic, shards(): pooled = jnp.mean(block_out, axis=(1, 2)).astype(jnp.bfloat16)  14.9 us
    dot_general x1, matrix products, shards(): lax.dot_general(pooled, class_w, (((1,), (1,)), ((), ())), preferred_elem...  6.09 us
    add x2, other arithmetic, blend_all(): return start_part + bend_part + final_part  5.52 us
    slice x1, local copies, waits for them, and re-layouts, spatial_conv(): padded[:, :, 0:side_len, :]  4.94 us
  transfers between devices with their start and end apart: 4, of which 2 were waited for; matrix products, arithmetic and copies ran while one was open for 42% of the time, Pallas kernels for 0%

commit v1 on v0

--- a/solution.py
+++ b/solution.py
@@ -4,6 +4,10 @@
 from jax.sharding import PartitionSpec as P
 
 EPSILON = 1e-05
+
+
+def cover_the_group(unit, peer_axis):
+    return jnp.concatenate(lax.all_gather(unit, peer_axis), axis=1)
 
 
 def curve_coefficients(t_values, point_index):
@@ -33,7 +37,7 @@
     if by_columns:
         gathered = lax.all_gather(endpoints, "point", axis=2, tiled=True)
     else:
-        gathered = lax.all_gather(endpoints, "point", axis=1, tiled=True)
+        gathered = cover_the_group(endpoints, "point")
     return blend_all(own_row, gathered)[0].astype(jnp.bfloat16)
 
 

time: 209 us -> 232 us (1.11)
  waiting for transfers between devices: 24.9 us -> 47.7 us
  matrix products: 57.1 us -> 50.5 us
  other arithmetic: 32.2 us -> 38.5 us
    all_gather x3, waiting for transfers between devices: 22.3 us -> 45.1 us  [cover_the_group(): return jnp.concatenate(lax.all_gather(unit, peer_axis), axis=1)]
    another operation x0 -> x3, other arithmetic: none -> 11 us
    dot_general x5, matrix products: 51 us -> 44.4 us  [map_product(): lax.dot_general(maps, kernel, (((3,), (0,)), ((), ())), preferred_element...]
    convert_element_type x1 -> x0, other arithmetic: 4.52 us -> none  [point_weight(): return blend_all(own_row, gathered)[0].astype(jnp.bfloat16)]
    all_gather x0 -> x1, local copies, waits for them, and re-layouts: none -> 2.39 us  [cover_the_group(): return jnp.concatenate(lax.all_gather(unit, peer_axis), axis=1)]
  transfers between devices with their start and end apart: 4 -> 4, of which waited for: 2 -> 3; matrix products, arithmetic and copies ran while one was open for 42% -> 39% of each run, Pallas kernels for 0% -> 0%
where the time goes in v1:
time: 232 us; the launch traced here: 231 us
  blocking collectives  71.6 us (31%)
  matrix products  50.5 us (22%)
  waiting for transfers between devices  47.7 us (21%)
  other arithmetic  38.5 us (17%)
  between operations  14.6 us (6%)
  local copies, waits for them, and re-layouts  8 us (3%)
    all_gather x3, waiting for transfers between devices, cover_the_group(): return jnp.concatenate(lax.all_gather(unit, peer_axis), axis=1)  45.1 us
    dot_general x5, matrix products, map_product(): lax.dot_general(maps, kernel, (((3,), (0,)), ((), ())), preferred_element...  44.4 us
    psum x1, blocking collectives, shards(): margin_all = lax.psum(placed, ('point', 'batch'))  39.5 us
    psum x3, blocking collectives, batch_norm(): lax.psum((jnp.sum(pre_norm, axis=(0, 1, 2)), jnp.sum(pre_norm * pre_norm,...  32.1 us
    reduce_sum x1, other arithmetic, shards(): pooled = jnp.mean(block_out, axis=(1, 2)).astype(jnp.bfloat16)  14.7 us
    another operation x3, other arithmetic  11 us
    dot_general x1, matrix products, shards(): lax.dot_general(pooled, class_w, (((1,), (1,)), ((), ())), preferred_elem...  6.11 us
    add x2, other arithmetic, blend_all(): return start_part + bend_part + final_part  5.56 us
  transfers between devices with their start and end apart: 4, of which 3 were waited for; matrix products, arithmetic and copies ran while one was open for 39% of the time, Pallas kernels for 0%

profile of v1, /device:TPU:0, one launch (start us, length us, event | category | flops | bytes accessed | tf_op | source)
XLA Modules:
  0.0 231.1 jit_solution(203467350426466594)
XLA Ops:
  7.9 0.7 all-gather.14.cloned.1.call-update
  10.0 0.9 select_reduce_fusion.2
  11.5 2.8 %multiply_add_fusion = (f32[1,1536]{1,0:T(1,128)S(1)}, f32[1,1536]{1,0:T(1,128)S(1)}) fusion(f32[3,1536]{1,0:T(4,128)} %param.20, f32[]{:T(128)} %bitcast.8, f32[]{:T(128)} %bitcast.6, f32[]{:T(128)} %bitcast.3, f32[3,1536]{1,0:T(4,128)} %param.19), kind=kLoop, calls=%fused_computation.36 | loop fusion | flops 15360 | bytes 49164 | tf_op jit(solution)/shard_map/add | solution.py:33
  14.3 2.8 %multiply_add_fusion.2 = f32[1,1000]{1,0:T(1,128)S(1)} fusion(f32[3,1000]{1,0:T(4,128)} %param.21, f32[]{:T(128)} %bitcast.8, f32[]{:T(128)} %bitcast.6, f32[]{:T(128)} %bitcast.3), kind=kLoop, calls=%fused_computation.38 | loop fusion | flops 5000 | bytes 16012 | tf_op jit(solution)/shard_map/add | solution.py:33
  17.1 21.1 %all-gather.10.cloned.1.call-done = bf16[24,128,256]{2,1,0:T(8,128)(2,1)} async-done(((bf16[3,128,256]{2,1,0:T(8,128)(2,1)}), bf16[24,128,256]{2,1,0:T(8,128)(2,1)}) %all-gather.10.cloned.1.call-update) | async-done | bytes 1572880 | tf_op jit(solution)/shard_map/all_gather | solution.py:10
  38.2 3.6 %add_convert_fusion.3 = bf16[1,8,128,256]{3,2,0,1:T(8,128)(2,1)S(1)} fusion(bf16[3,8,128,256]{3,2,0,1:T(8,128)(2,1)} %bitcast.75, f32[]{:T(128)} %bitcast.8, f32[]{:T(128)} %bitcast.6, f32[]{:T(128)} %bitcast.3), kind=kLoop, calls=%fused_computation.25 | loop fusion | flops 2359296 | bytes 2097164 | tf_op jit(solution)/shard_map/convert.2
  41.8 10.8 %multiply_reduce_fusion.2 = (f32[256]{0:T(256)S(1)}, f32[256]{0:T(256)S(1)}, f32[256,32,14,14]{0,1,3,2:T(8,128)}) fusion(bf16[1024,256,1,1]{1,0,3,2:T(8,128)(2,1)S(1)} %bitcast.80, bf16[32,14,14,1024]{3,0,2,1:T(8,128)(2,1)} %param.11), kind=kOutput, calls=%fused_computation.7 | convolution fusion | flops 3293150720 | bytes 19793920 | tf_op jit(solution)/shard_map/dot_general | solution.py:45
  52.6 11.7 %all-reduce.3 = (f32[256]{0:T(256)S(1)}, f32[256]{0:T(256)S(1)}) all-reduce(f32[256]{0:T(256)S(1)} %get-tuple-element.12, f32[256]{0:T(256)S(1)} %get-tuple-element.11), channel_id=1, replica_groups=mesh['point'=8,'batch'=4] {'batch'}, use_global_device_ids=true, to_apply=%region_2.3 | all-reduce | flops 512 | bytes 4096 | tf_op jit(solution)/shard_map/psum | solution.py:51
  64.8 0.8 all-gather.14.cloned.1.call-done
  65.7 3.6 %add_convert_fusion.2 = bf16[1,8,32,1024]{3,2,0,1:T(8,128)(2,1)S(1)} fusion(bf16[3,8,32,1024]{3,2,0,1:T(8,128)(2,1)} %bitcast.74, f32[]{:T(128)} %bitcast.8, f32[]{:T(128)} %bitcast.6, f32[]{:T(128)} %bitcast.3), kind=kLoop, calls=%fused_computation.24 | loop fusion | flops 2359296 | bytes 2097164 | tf_op jit(solution)/shard_map/convert
  69.3 4.1 %fusion.1 = bf16[32,14,14,256]{3,0,2,1:T(8,128)(2,1)S(1)} fusion(f32[256,32,14,14]{0,1,3,2:T(8,128)} %get-tuple-element.43, f32[256]{0:T(256)S(1)} %bitcast.85, f32[256]{0:T(256)S(1)} %bitcast.86, f32[256]{0:T(256)S(1)} %get-tuple-element.25, f32[256]{0:T(256)S(1)} %get-tuple-element.39), kind=kLoop, calls=%fused_computation.14 | loop fusion | flops 9633792 | bytes 9637888 | tf_op jit(solution)/shard_map/convert_element_type | solution.py:107
  73.3 4.9 %pad_slice_fusion.2 = (bf16[32,16,14,256]{3,0,2,1:T(8,128)(2,1)}, bf16[32,16,14,256]{3,0,2,1:T(8,128)(2,1)}, bf16[32,16,14,256]{3,0,2,1:T(8,128)(2,1)}) fusion(bf16[32,14,14,256]{3,0,2,1:T(8,128)(2,1)S(1)} %fusion.1), kind=kLoop, calls=%fused_computation.10 | loop fusion | bytes 14221312 | tf_op jit(solution)/shard_map/slice | solution.py:66
  78.3 23.2 %all-gather.12.cloned.1.call-done = bf16[24,288,256]{2,1,0:T(8,128)(2,1)} async-done(((bf16[3,288,256]{2,1,0:T(8,128)(2,1)}), bf16[24,288,256]{2,1,0:T(8,128)(2,1)}) %all-gather.12.cloned.1.call-update) | async-done | bytes 3538960 | tf_op jit(solution)/shard_map/all_gather | solution.py:10
  101.4 2.4 %copy.27 = bf16[8,3,288,256]{3,2,0,1:T(8,128)(2,1)S(1)} copy(bf16[8,3,288,256]{3,2,1,0:T(8,128)(2,1)} %bitcast.73) | data formatting | bytes 7077888 | tf_op jit(solution)/shard_map/all_gather | solution.py:10
  103.8 3.8 %add_convert_fusion.1 = bf16[1,8,288,256]{3,2,1,0:T(8,128)(2,1)S(1)} fusion(bf16[3,8,288,256]{3,2,1,0:T(8,128)(2,1)S(1)} %bitcast.72, f32[]{:T(128)} %bitcast.8, f32[]{:T(128)} %bitcast.6, f32[]{:T(128)} %bitcast.3), kind=kLoop, calls=%fused_computation.20 | loop fusion | flops 5308416 | bytes 4718604 | tf_op jit(solution)/shard_map/convert.1
  107.7 5.3 %fusion.14 = f32[32,14,14,256]{3,0,2,1:T(8,128)} fusion(bf16[2304,256]{1,0:T(8,128)(2,1)S(1)} %bitcast.76, bf16[32,16,14,256]{3,0,2,1:T(8,128)(2,1)S(1)} %copy-done.2, bf16[32,16,14,256]{3,0,2,1:T(8,128)(2,1)S(1)} %copy-done.1, bf16[32,16,14,256]{3,0,2,1:T(8,128)(2,1)S(1)} %copy-done), kind=kOutput, calls=%fused_computation.30 | convolution fusion | flops 2499280896 | bytes 17825792 | tf_op jit(solution)/shard_map/dot_general | solution.py:45
  113.0 5.4 %fusion.13 = f32[32,14,14,256]{3,0,2,1:T(8,128)} fusion(bf16[2304,256]{1,0:T(8,128)(2,1)S(1)} %bitcast.77, bf16[32,16,14,256]{3,0,2,1:T(8,128)(2,1)S(1)} %copy-done.2, bf16[32,16,14,256]{3,0,2,1:T(8,128)(2,1)S(1)} %copy-done.1, bf16[32,16,14,256]{3,0,2,1:T(8,128)(2,1)S(1)} %copy-done), kind=kOutput, calls=%fused_computation.28 | convolution fusion | flops 2499280896 | bytes 17825792 | tf_op jit(solution)/shard_map/dot_general | solution.py:45
  118.3 8.9 %multiply_reduce_fusion.1 = (f32[256]{0:T(256)S(1)}, f32[256]{0:T(256)S(1)}, f32[32,14,14,256]{3,0,2,1:T(8,128)}) fusion(bf16[2304,256]{1,0:T(8,128)(2,1)S(1)} %bitcast.78, bf16[32,16,14,256]{3,0,2,1:T(8,128)(2,1)S(1)} %copy-done.2, bf16[32,16,14,256]{3,0,2,1:T(8,128)(2,1)S(1)} %copy-done.1, bf16[32,16,14,256]{3,0,2,1:T(8,128)(2,1)S(1)} %copy-done, ...), kind=kOutput, calls=%fused_computation.5 | convolution fusion | flops 2507308544 | bytes 30672896 | tf_op jit(solution)/shard_map/dot_general | solution.py:45
  127.3 11.8 %all-reduce.2 = (f32[256]{0:T(256)S(1)}, f32[256]{0:T(256)S(1)}) all-reduce(f32[256]{0:T(256)S(1)} %get-tuple-element.10, f32[256]{0:T(256)S(1)} %get-tuple-element.9), channel_id=1, replica_groups=mesh['point'=8,'batch'=4] {'batch'}, use_global_device_ids=true, to_apply=%region_6.7 | all-reduce | flops 512 | bytes 4096 | tf_op jit(solution)/shard_map/psum | solution.py:51
  139.7 14.0 %multiply_reduce_fusion = (f32[1024]{0:T(1024)S(1)}, f32[1024]{0:T(1024)S(1)}, f32[32,14,14,1024]{3,0,2,1:T(8,128)}) fusion(bf16[256,1024,1,1]{1,0,3,2:T(8,128)(2,1)S(1)} %bitcast.79, f32[32,14,14,256]{3,0,2,1:T(8,128)} %get-tuple-element.44, f32[256]{0:T(256)S(1)} %bitcast.92, f32[256]{0:T(256)S(1)} %bitcast.93, f32[256]{0:T(256)S(1)} %get-tuple-element.23, ...), kind=kOutput, calls=%fused_computation.1 | convolution fusion | flops 3317233664 | bytes 32649216 | tf_op jit(solution)/shard_map/dot_general | solution.py:45
  153.7 8.6 %all-reduce.1 = (f32[1024]{0:T(1024)S(1)}, f32[1024]{0:T(1024)S(1)}) all-reduce(f32[1024]{0:T(1024)S(1)} %get-tuple-element.8, f32[1024]{0:T(1024)S(1)} %get-tuple-element.7), channel_id=1, replica_groups=mesh['point'=8,'batch'=4] {'batch'}, use_global_device_ids=true, to_apply=%region_10.11 | all-reduce | flops 2048 | bytes 16384 | tf_op jit(solution)/shard_map/psum | solution.py:51
  162.9 14.7 %maximum_reduce_fusion = f32[32,1024]{1,0:T(8,128)S(1)} fusion(bf16[32,14,14,1024]{3,0,2,1:T(8,128)(2,1)} %param.11, f32[32,14,14,1024]{3,0,2,1:T(8,128)} %get-tuple-element.45, f32[1024]{0:T(1024)S(1)} %bitcast.82, f32[1024]{0:T(1024)S(1)} %bitcast.83, f32[1024]{0:T(1024)S(1)} %get-tuple-element.21, f32[1024]{0:T(1024)S(1)} %get-tuple-element.34), kind=kLoop, calls=%fused_computation | loop fusion | flops 51347456 | bytes 38682624 | tf_op jit(solution)/shard_map/reduce_sum | solution.py:118
  177.7 6.1 %select_reduce_fusion = (f32[32]{0:T(128)S(1)}, f32[32]{0:T(128)S(1)}) fusion(s32[32]{0:T(128)S(1)} %copy-done.6, f32[1000]{0:T(1024)S(1)} %bitcast.88, bf16[3,1000,1024]{2,1,0:T(8,128)(2,1)} %all-gather.8.cloned.1.call-done, f32[]{:T(128)} %bitcast.8, f32[]{:T(128)} %bitcast.6, f32[]{:T(128)} %bitcast.3, f32[32,1024]{1,0:T(8,128)S(1)} %maximum_reduce_fusion), kind=kOutput, calls=%fused_computation.31 | convolution fusion | flops 75009472 | bytes 6279468 | tf_op jit(solution)/shard_map/dot_general | solution.py:120
  185.1 39.5 %psum.55 = f32[8]{0:T(128)} all-reduce(f32[8]{0:T(128)S(1)} %compare_select_fusion), channel_id=1, replica_groups=mesh['point'=8,'batch'=4] {'point','batch'}, use_global_device_ids=true, to_apply=%region_17.18 | all-reduce | flops 8 | bytes 64 | tf_op jit(solution)/shard_map/psum | solution.py:134
  (35 shorter events, 5.1 us)
Async XLA Ops:
  7.2 31.0 %all-gather.10.cloned.1.call-start = ((), (), s32[]{:S(2)}) async-start(), calls=%async_computation.1 | async-start | bytes 1769472 | tf_op jit(solution)/shard_map/all_gather | solution.py:10
  7.9 57.8 %all-gather.14.cloned.1.call-start = ((), (), s32[]{:S(2)}) async-start(), calls=%async_computation.3 | async-start | bytes 1769472 | tf_op jit(solution)/shard_map/all_gather | solution.py:10
  8.7 92.8 %all-gather.12.cloned.1.call-start = ((), (), s32[]{:S(2)}) async-start(), calls=%async_computation.2 | async-start | bytes 3981312 | tf_op jit(solution)/shard_map/all_gather | solution.py:10
  9.4 168.3 %all-gather.8.cloned.1.call-start = ((), (), s32[]{:S(2)}) async-start(), calls=%async_computation | async-start | bytes 6912000 | tf_op jit(solution)/shard_map/all_gather | solution.py:38
  64.8 13.4 %copy-start.4 = (f32[256]{0:T(256)}, f32[256]{0:T(256)S(1)}, u32[]{:S(2)}) copy-start(f32[256]{0:T(256)S(1)} %get-tuple-element.39) | copy-start | bytes 3076
  101.4 6.2 %copy-start = (bf16[32,16,14,256]{3,0,2,1:T(8,128)(2,1)S(1)}, bf16[32,16,14,256]{3,0,2,1:T(8,128)(2,1)}, u32[]{:S(2)}) copy-start(bf16[32,16,14,256]{3,0,2,1:T(8,128)(2,1)} %get-tuple-element.27) | copy-start | bytes 11010052
  101.4 6.2 %copy-start.1 = (bf16[32,16,14,256]{3,0,2,1:T(8,128)(2,1)S(1)}, bf16[32,16,14,256]{3,0,2,1:T(8,128)(2,1)}, u32[]{:S(2)}) copy-start(bf16[32,16,14,256]{3,0,2,1:T(8,128)(2,1)} %get-tuple-element.28) | copy-start | bytes 11010052
  101.4 6.2 %copy-start.2 = (bf16[32,16,14,256]{3,0,2,1:T(8,128)(2,1)S(1)}, bf16[32,16,14,256]{3,0,2,1:T(8,128)(2,1)}, u32[]{:S(2)}) copy-start(bf16[32,16,14,256]{3,0,2,1:T(8,128)(2,1)} %get-tuple-element.29) | copy-start | bytes 11010052
  139.7 14.0 %copy-start.5 = (f32[256]{0:T(256)}, f32[256]{0:T(256)S(1)}, u32[]{:S(2)}) copy-start(f32[256]{0:T(256)S(1)} %get-tuple-element.38) | copy-start | bytes 3076
  162.9 14.8 %copy-start.3 = (f32[1024]{0:T(1024)}, f32[1024]{0:T(1024)S(1)}, u32[]{:S(2)}) copy-start(f32[1024]{0:T(1024)S(1)} %get-tuple-element.34) | copy-start | bytes 12292
  162.9 14.8 %copy-start.6 = (s32[32]{0:T(128)S(1)}, s32[32]{0:T(128)}, u32[]{:S(2)}) copy-start(s32[32]{0:T(128)} %param.12) | copy-start | bytes 388
Sparse Core Ops, SparseCore 0:
  9.9 28.2 all-gather.9
  40.1 25.5 all-gather.13
  67.6 33.8 all-gather.11
  103.2 45.9 all-gather.7
